TPU v7x, 256 devices: a whole 4x4x8 slice. The times are simulated.
256 devices in a mesh: dp: 8 (over y, core), expert: 32 (over x, z).
Axes of the slice: x: 4, y: 4, z: 8, core: 2. Of those that a mesh axis runs over, the one named last changes fastest.
Arguments:
- tokens: bfloat16 [32768, 2048], P(('dp', 'expert')), may hold values from -6 to 6
- expert_ids: int32 [32768, 2], P(('dp', 'expert')), may hold values from 0 to 31, all different within a row; in each aligned block of 128 rows (0 to 127, 128 to 255, ...) at most 12 rows name the same one
- upstream: bfloat16 [32768, 2048], P(('dp', 'expert')), may hold values from -6 to 6
- gain: float32 [2048], replicated, may hold values from 0.5 to 1.5
- router: bfloat16 [2048, 32], replicated, may hold values from -0.125 to 0.125
- gate_weight_matrix: bfloat16 [32, 2048, 1024], P('expert', 'dp'), may hold values from -0.125 to 0.125
- up_weight: bfloat16 [32, 2048, 1024], P('expert', 'dp'), may hold values from -0.125 to 0.125
- down_weight: bfloat16 [32, 1024, 2048], P('expert', None, 'dp'), may hold values from -0.1875 to 0.1875
Outputs:
- mixed: bfloat16 [32768, 2048], P(('dp', 'expert'))
- d_tokens: bfloat16 [32768, 2048], P(('dp', 'expert'))
- gate_weight_gradient: bfloat16 [32, 2048, 1024], P('expert', 'dp')
- up_weight_gradient: bfloat16 [32, 2048, 1024], P('expert', 'dp')
- down_weight_gradient: bfloat16 [32, 1024, 2048], P('expert', None, 'dp')
- d_router: float32 [2048, 32], replicated
- d_gain: float32 [2048], replicated
Inputs may be any that keep to these rules, and one draw needn't show every extreme that they name: `expert_ids`: the two experts of a token differ. Among the tokens of one device (aligned blocks of 128 rows) no expert is named more than 12 times, and in some block one expert is named exactly 12 times.
All inputs are finite; a program needn't handle non-finite values.
Results may differ from a plain program's by a relative error of at most 0.014.
Values may be sent and summed in bfloat16 or wider, within the bound.
No kernel may reach another device: no remote copies, remote signals or barrier semaphores. Data moves between devices by JAX's collectives and lax.ppermute only.
A program may use at most 128 MiB of HBM per device.

v0:
```python
import jax
import jax.numpy as jnp
from jax import lax
from jax.sharding import PartitionSpec as P

norm_eps = 1e-06


def slot_layout(expert_ids, experts, capacity):
    flattened = expert_ids.reshape(-1)
    onehot = (flattened[:, None] == jnp.arange(experts, dtype=jnp.int32)[None, :]).astype(jnp.int32)
    ranking = jnp.sum(jnp.cumsum(onehot, axis=0) * onehot, axis=1) - 1
    slot_ids = flattened * capacity + ranking
    sources = (
        jnp.zeros((experts * capacity,), jnp.int32)
        .at[slot_ids]
        .set(jnp.arange(flattened.shape[0], dtype=jnp.int32))
    )
    counts = jnp.sum(onehot, axis=0)
    slots_occupied = (jnp.arange(capacity, dtype=jnp.int32)[None, :] < counts[:, None]).reshape(-1)
    return (slot_ids, sources, slots_occupied)


def transposed_product(left, right):
    return lax.dot_general(
        left, right, (((1,), (1,)), ((), ())), preferred_element_type=jnp.float32
    )


def inner_product(left, right):
    return lax.dot_general(
        left, right, (((0,), (0,)), ((), ())), preferred_element_type=jnp.float32
    )


def on_device(
    tokens, expert_ids, upstream, gain, router, gate_weight_matrix, up_weight, down_weight
):
    experts = lax.axis_size("expert")
    tok_rows = tokens.shape[0]
    width = tokens.shape[1]
    feed = gate_weight_matrix.shape[2]
    capacity = 3 * tok_rows // experts
    source = tokens.astype(jnp.float32)
    inverse = lax.rsqrt(jnp.mean(source * source, axis=-1, keepdims=True) + norm_eps)
    unit_rows = source * inverse
    normed = (unit_rows * gain).astype(jnp.bfloat16)
    scores = jax.nn.sigmoid(jnp.dot(normed, router, preferred_element_type=jnp.float32))
    picked = expert_ids[:, :, None] == jnp.arange(experts, dtype=jnp.int32)[None, None, :]
    chosen = jnp.sum(jnp.where(picked, scores[:, None, :], 0.0), axis=2)
    total = jnp.sum(chosen, axis=1, keepdims=True)
    gates = chosen / total
    slot_ids, sources, slots_occupied = slot_layout(expert_ids, experts, capacity)
    slot_pairs = slot_ids.reshape(tok_rows, 2)
    send_rows = jnp.where(
        slots_occupied[:, None], normed[sources // 2], jnp.zeros((), jnp.bfloat16)
    )
    arrived = lax.all_to_all(
        send_rows.reshape(experts, capacity, width),
        "expert",
        split_axis=0,
        concat_axis=0,
        tiled=True,
    )
    expert_in = arrived.reshape(experts * capacity, width)
    pieces = (
        lax.all_gather(gate_weight_matrix, "dp", axis=1, tiled=True),
        lax.all_gather(up_weight, "dp", axis=1, tiled=True),
    )
    columns = expert_in
    pre_gate = jnp.dot(columns, pieces[0][0], preferred_element_type=jnp.float32)
    pre_up = jnp.dot(columns, pieces[1][0], preferred_element_type=jnp.float32)
    sigma = jax.nn.sigmoid(pre_gate)
    active = pre_gate * sigma
    hidden = (active * pre_up).astype(jnp.bfloat16)
    expert_out = jnp.dot(
        hidden,
        lax.all_gather(down_weight, "dp", axis=2, tiled=True)[0],
        preferred_element_type=jnp.float32,
    ).astype(jnp.bfloat16)
    returned = lax.all_to_all(
        expert_out.reshape(experts, capacity, width),
        "expert",
        split_axis=0,
        concat_axis=0,
        tiled=True,
    )
    outputs = returned.reshape(experts * capacity, width)[slot_pairs].astype(jnp.float32)
    combined = gates[:, :, None] * outputs
    mixed = (source + combined[:, 0] + combined[:, 1]).astype(jnp.bfloat16)
    cotangent = upstream.astype(jnp.float32)
    d_gates = jnp.sum(cotangent[:, None, :] * outputs, axis=2)
    weight_rows = gates.reshape(-1)[sources]
    d_send = jnp.where(
        slots_occupied[:, None], weight_rows[:, None] * cotangent[sources // 2], 0.0
    ).astype(jnp.bfloat16)
    d_arrived = lax.all_to_all(
        d_send.reshape(experts, capacity, width), "expert", split_axis=0, concat_axis=0, tiled=True
    )
    d_out = d_arrived.reshape(experts * capacity, width)
    columns = d_out
    d_hidden = transposed_product(columns, lax.all_gather(down_weight, "dp", axis=2, tiled=True)[0])
    d_pre_gate = (d_hidden * pre_up * sigma * (1.0 + pre_gate * (1.0 - sigma))).astype(jnp.bfloat16)
    d_pre_up = (d_hidden * active).astype(jnp.bfloat16)
    pieces = (
        lax.all_gather(gate_weight_matrix, "dp", axis=1, tiled=True),
        lax.all_gather(up_weight, "dp", axis=1, tiled=True),
    )
    block = transposed_product(d_pre_gate, pieces[0][0]) + transposed_product(
        d_pre_up, pieces[1][0]
    )
    d_rows = block.astype(jnp.bfloat16)
    d_back = lax.all_to_all(
        d_rows.reshape(experts, capacity, width), "expert", split_axis=0, concat_axis=0, tiled=True
    )
    d_parts = d_back.reshape(experts * capacity, width)[slot_pairs].astype(jnp.float32)
    grad_rows = lax.psum_scatter(
        jnp.concatenate(
            [
                inner_product(expert_in, d_pre_gate),
                inner_product(expert_in, d_pre_up),
                inner_product(d_out, hidden),
            ],
            axis=1,
        ).astype(jnp.bfloat16),
        "dp",
        scatter_dimension=0,
        tiled=True,
    ).astype(jnp.float32)
    gate_weight_gradient = grad_rows[:, :feed].astype(jnp.bfloat16)[None]
    up_weight_gradient = grad_rows[:, feed : 2 * feed].astype(jnp.bfloat16)[None]
    down_weight_gradient = grad_rows[:, 2 * feed :].T.astype(jnp.bfloat16)[None]
    blended = jnp.sum(gates * d_gates, axis=1, keepdims=True)
    d_chosen = (d_gates - blended) / total
    d_logit = d_chosen * chosen * (1.0 - chosen)
    d_logits = jnp.sum(jnp.where(picked, d_logit[:, :, None], 0.0), axis=1)
    router_float = router.astype(jnp.float32)
    d_normed = (
        d_parts[:, 0]
        + d_parts[:, 1]
        + jnp.dot(d_logits, router_float.T, precision=lax.Precision.HIGHEST)
    )
    d_unit = d_normed * gain
    inner = jnp.mean(d_unit * unit_rows, axis=-1, keepdims=True)
    d_tokens = (cotangent + inverse * (d_unit - unit_rows * inner)).astype(jnp.bfloat16)
    part_router = jnp.dot(normed.astype(jnp.float32).T, d_logits, precision=lax.Precision.HIGHEST)
    part_gain = jnp.sum(d_normed * unit_rows, axis=0)
    d_router, d_gain = lax.psum((part_router, part_gain), ("dp", "expert"))
    return (
        mixed,
        d_tokens,
        gate_weight_gradient,
        up_weight_gradient,
        down_weight_gradient,
        d_router,
        d_gain,
    )


def solution(mesh):
    return jax.shard_map(
        on_device,
        mesh=mesh,
        in_specs=(
            P(("dp", "expert"), None),
            P(("dp", "expert"), None),
            P(("dp", "expert"), None),
            P(),
            P(),
            P("expert", "dp", None),
            P("expert", "dp", None),
            P("expert", None, "dp"),
        ),
        out_specs=(
            P(("dp", "expert"), None),
            P(("dp", "expert"), None),
            P("expert", "dp", None),
            P("expert", "dp", None),
            P("expert", None, "dp"),
            P(),
            P(),
        ),
        check_vma=False,
    )
```

profile of v0, /device:TPU:2, one launch (start us, length us, event | category | flops | bytes accessed | tf_op | source)
XLA Modules:
  0.0 638.8 jit_solution(4836383149556349928)
XLA Ops:
  13.7 3.1 gather_fusion
  16.8 2.4 gather.20
  19.5 60.0 %all_to_all.20 = bf16[32,12,2048]{2,1,0:T(8,128)(2,1)S(1)} all-to-all(bf16[32,12,2048]{2,1,0:T(8,128)(2,1)S(1)} %broadcast_select_fusion), channel_id=1, replica_groups=mesh['dp'=8,'expert'=32] {'expert'}, dimensions={0} | all-to-all | bytes 3145728 | tf_op jit(solution)/shard_map/all_to_all | solution.py:58
  80.9 5.8 fusion.10
  86.6 5.9 multiply_convert_fusion.2
  92.6 31.3 %all-gather.8.cloned.1.call-done = bf16[1,1024,2048]{2,1,0:T(8,128)(2,1)} async-done(((bf16[1,1024,256]{2,1,0:T(8,128)(2,1)}), bf16[1,1024,2048]{2,1,0:T(8,128)(2,1)}) %all-gather.8.cloned.1.call-update) | async-done | bytes 4194320 | tf_op jit(solution)/shard_map/all_gather | solution.py:78
  123.9 4.2 fusion.14
  129.7 10.3 %all-to-all-start.1 = ((bf16[32,12,2048]{2,1,0:T(8,128)(2,1)}), bf16[32,12,2048]{2,1,0:T(8,128)(2,1)}, u32[]{:S(2)}, u32[]{:S(2)}) async-start(bf16[32,12,2048]{2,1,0:T(8,128)(2,1)} %reshape.197), calls=%async_computation.1 | async-start | bytes 4194304 | tf_op jit(solution)/shard_map/all_to_all | solution.py:81
  140.6 3.3 gather_fusion.3
  143.9 4.6 gather.24
  148.9 39.2 %all-to-all-done.1 = bf16[32,12,2048]{2,1,0:T(8,128)(2,1)} async-done(((bf16[32,12,2048]{2,1,0:T(8,128)(2,1)}), bf16[32,12,2048]{2,1,0:T(8,128)(2,1)}, u32[]{:S(2)}, u32[]{:S(2)}) %all-to-all-start.1) | async-done | bytes 1572896 | tf_op jit(solution)/shard_map/all_to_all | solution.py:81
  188.1 2.5 reshape.198
  190.6 2.4 gather_fusion.1
  193.0 3.4 reshape.257
  196.3 2.6 multiply_reduce_fusion
  199.3 2.8 gather_fusion.2
  202.2 2.6 select_convert_fusion
  204.9 57.8 %all_to_all.21 = bf16[32,12,2048]{2,1,0:T(8,128)(2,1)S(1)} all-to-all(bf16[32,12,2048]{2,1,0:T(8,128)(2,1)S(1)} %select_convert_fusion), channel_id=1, replica_groups=mesh['dp'=8,'expert'=32] {'expert'}, dimensions={0} | all-to-all | bytes 3145728 | tf_op jit(solution)/shard_map/all_to_all | solution.py:97
  264.0 4.1 convolution_convert_fusion
  268.3 2.3 multiply_convert_fusion.1
  270.6 2.4 convolution_convert_fusion.2
  273.0 2.4 convolution_convert_fusion.1
  275.4 21.4 %pad_maximum_fusion = bf16[2048,3072]{0,1:T(8,128)(2,1)} fusion(bf16[2048,1024]{0,1:T(8,128)(2,1)S(1)} %convolution_convert_fusion, bf16[2048,1024]{0,1:T(8,128)(2,1)S(1)} %convolution_convert_fusion.1, bf16[2048,1024]{0,1:T(8,128)(2,1)S(1)} %convolution_convert_fusion.2), kind=kLoop, calls=%fused_computation.6 | loop fusion | flops 37748736 | bytes 25165824 | tf_op jit(solution)/shard_map/concatenate | solution.py:118
  297.9 4.2 fusion.4
  305.5 7.8 %all-to-all-start.3 = ((bf16[32,12,2048]{2,1,0:T(8,128)(2,1)}), bf16[32,12,2048]{2,1,0:T(8,128)(2,1)}, u32[]{:S(2)}, u32[]{:S(2)}) async-start(bf16[32,12,2048]{2,1,0:T(8,128)(2,1)} %reshape.200), calls=%async_computation.3 | async-start | bytes 4194304 | tf_op jit(solution)/shard_map/all_to_all | solution.py:113
  314.4 2.6 copy_multiply_fusion
  317.0 43.3 %all-to-all-done.3 = bf16[32,12,2048]{2,1,0:T(8,128)(2,1)} async-done(((bf16[32,12,2048]{2,1,0:T(8,128)(2,1)}), bf16[32,12,2048]{2,1,0:T(8,128)(2,1)}, u32[]{:S(2)}, u32[]{:S(2)}) %all-to-all-start.3) | async-done | bytes 1572896 | tf_op jit(solution)/shard_map/all_to_all | solution.py:113
  360.3 2.7 reshape.201
  367.4 2.3 fusion.31
  369.7 74.9 %psum.15 = f32[2048]{0:T(1024)} all-reduce(f32[2048]{0:T(1024)S(1)} %get-tuple-element.35), channel_id=1, replica_groups=mesh['dp'=8,'expert'=32] {'dp','expert'}, use_global_device_ids=true, to_apply=%region_15.16 | all-reduce | flops 2048 | bytes 16384 | tf_op jit(solution)/shard_map/psum | solution.py:148
  444.7 2.7 fusion.30
  451.7 178.7 %all-reduce.2.cloned.1.call-done = f32[2048,32]{0,1:T(8,128)} async-done(((f32[2048,32]{0,1:T(8,128)}), f32[2048,32]{0,1:T(8,128)}) %all-reduce.2.cloned.1.call-update) | async-done | bytes 262160 | tf_op jit(solution)/shard_map/psum | solution.py:148
  (102 shorter events, 28.3 us)
Async XLA Ops:
  7.2 141.4 %copy-start = (bf16[2048,32]{0,1:T(8,128)(2,1)S(1)}, bf16[2048,32]{0,1:T(8,128)(2,1)}, u32[]{:S(2)}) copy-start(bf16[2048,32]{0,1:T(8,128)(2,1)} %param.12) | copy-start | bytes 393220
  7.2 6.1 copy-start.3
  7.2 6.3 copy-start.10
  7.2 73.7 %all-gather.4.cloned.1.call-start = ((), (), s32[]{:S(2)}) async-start(), calls=%async_computation.5 | async-start | bytes 4718592 | tf_op jit(solution)/shard_map/all_gather | solution.py:67
  7.9 78.7 %all-gather.6.cloned.1.call-start = ((), (), s32[]{:S(2)}) async-start(), calls=%async_computation.6 | async-start | bytes 4718592 | tf_op jit(solution)/shard_map/all_gather | solution.py:68
  8.7 115.2 %all-gather.8.cloned.1.call-start = ((), (), s32[]{:S(2)}) async-start(), calls=%async_computation.7 | async-start | bytes 4718592 | tf_op jit(solution)/shard_map/all_gather | solution.py:78
  80.9 5.8 copy-start.7
  129.7 10.8 %copy-start.5 = (bf16[128,2048]{1,0:T(8,128)(2,1)S(1)}, bf16[128,2048]{1,0:T(8,128)(2,1)}, u32[]{:S(2)}) copy-start(bf16[128,2048]{1,0:T(8,128)(2,1)} %param.10) | copy-start | bytes 1572868
  129.7 58.4 %all-to-all-start.1 = ((bf16[32,12,2048]{2,1,0:T(8,128)(2,1)}), bf16[32,12,2048]{2,1,0:T(8,128)(2,1)}, u32[]{:S(2)}, u32[]{:S(2)}) async-start(bf16[32,12,2048]{2,1,0:T(8,128)(2,1)} %reshape.197), calls=%async_computation.1 | async-start | bytes 4194304 | tf_op jit(solution)/shard_map/all_to_all | solution.py:81
  140.0 307.4 %reduce-scatter.2.cloned.1.call-start = ((), (), s32[]{:S(2)}) async-start(), calls=%async_computation.8 | async-start | bytes 14155776 | tf_op jit(solution)/shard_map/reduce_scatter | solution.py:117
  143.9 4.9 copy-start.11
  264.0 4.2 copy-start.9
  264.0 4.2 copy-start.13
  264.0 4.2 copy-start.18
  264.0 4.3 copy-start.19
  268.3 2.3 copy-start.8
  270.5 2.4 copy-start.14
  270.6 2.4 copy-start.16
  296.8 1.1 copy-start.17
  297.9 4.2 copy-start.12
  297.9 4.2 copy-start.15
  305.5 8.9 %copy-start.1 = (f32[128,2,2048]{2,1,0:T(2,128)S(1)}, f32[128,2,2048]{2,1,0:T(2,128)}, u32[]{:S(2)}) copy-start(f32[128,2,2048]{2,1,0:T(2,128)} %reshape.257) | copy-start | bytes 6291460
  305.5 54.9 %all-to-all-start.3 = ((bf16[32,12,2048]{2,1,0:T(8,128)(2,1)}), bf16[32,12,2048]{2,1,0:T(8,128)(2,1)}, u32[]{:S(2)}, u32[]{:S(2)}) async-start(bf16[32,12,2048]{2,1,0:T(8,128)(2,1)} %reshape.200), calls=%async_computation.3 | async-start | bytes 4194304 | tf_op jit(solution)/shard_map/all_to_all | solution.py:113
  313.3 317.1 %all-reduce.2.cloned.1.call-start = ((), (), s32[]{:S(2)}) async-start(), calls=%async_computation.9 | async-start | bytes 524288 | tf_op jit(solution)/shard_map/psum | solution.py:148
  365.8 1.7 copy-start.4
  367.4 77.3 %copy-start.2 = (f32[128,2,2048]{2,0,1:T(8,128)S(1)}, f32[128,2,2048]{2,0,1:T(8,128)}, u32[]{:S(2)}) copy-start(f32[128,2,2048]{2,0,1:T(8,128)} %copy_multiply_fusion) | copy-start | bytes 6291460
  367.4 77.3 %copy-start.6 = (bf16[128,2048]{1,0:T(8,128)(2,1)S(1)}, bf16[128,2048]{1,0:T(8,128)(2,1)}, u32[]{:S(2)}) copy-start(bf16[128,2048]{1,0:T(8,128)(2,1)} %param.10) | copy-start | bytes 1572868
Sparse Core Ops, SparseCore 0:
  9.9 37.5 all-gather.3
  49.3 34.5 all-gather.5
  85.8 38.0 all-gather.7
  296.9 73.3 reduce-scatter.1
  376.2 254.0 all-reduce.1
where the time goes:
time: 646 us; the launch traced here: 639 us
  waiting for transfers between devices  295 us (46%)
  blocking collectives  193 us (30%)
  local copies, waits for them, and re-layouts  48 us (7%)
  matrix products  36.7 us (6%)
  other arithmetic  33.7 us (5%)
  starting transfers between devices  18.6 us (3%)
  between operations  14.5 us (2%)
    psum x1, waiting for transfers between devices, on_device(): d_router, d_gain = lax.psum((part_router, part_gain), ('dp', 'expert'))  179 us
    psum x1, blocking collectives, on_device(): d_router, d_gain = lax.psum((part_router, part_gain), ('dp', 'expert'))  74.9 us
    all_to_all x1, blocking collectives, on_device(): lax.all_to_all(send_rows.reshape(experts, capacity, width), 'expert', spl...  60 us
    all_to_all x1, blocking collectives, on_device(): lax.all_to_all(d_send.reshape(experts, capacity, width), 'expert', split_...  57.8 us
    all_to_all x1, waiting for transfers between devices, on_device(): lax.all_to_all(d_rows.reshape(experts, capacity, width), 'expert', split_...  43.3 us
    all_to_all x1, waiting for transfers between devices, on_device(): lax.all_to_all(expert_out.reshape(experts, capacity, width), 'expert', sp...  39.2 us
    all_gather x1, waiting for transfers between devices, on_device(): lax.all_gather(down_weight, 'dp', axis=2, tiled=True)[0]  31.3 us
    concatenate x1, other arithmetic, on_device(): jnp.concatenate([inner_product(expert_in, d_pre_gate), inner_product(expe...  21.4 us
  transfers between devices with their start and end apart: 7, of which 4 were waited for; matrix products, arithmetic and copies ran while one was open for 9% of the time, Pallas kernels for 0%

commit v1 on v0

--- a/solution.py
+++ b/solution.py
@@ -145,7 +145,7 @@
     d_tokens = (cotangent + inverse * (d_unit - unit_rows * inner)).astype(jnp.bfloat16)
     part_router = jnp.dot(normed.astype(jnp.float32).T, d_logits, precision=lax.Precision.HIGHEST)
     part_gain = jnp.sum(d_normed * unit_rows, axis=0)
-    d_router, d_gain = lax.psum((part_router, part_gain), ("dp", "expert"))
+    d_router, d_gain = lax.psum(lax.psum((part_router, part_gain), "expert"), "dp")
     return (
         mixed,
         d_tokens,

time: 646 us -> 534 us (0.83)
  waiting for transfers between devices: 295 us -> 228 us
  blocking collectives: 193 us -> 136 us
  starting transfers between devices: 18.6 us -> 29.3 us
    psum x1 -> x2, waiting for transfers between devices: 179 us -> 108 us  [the longest x1 56.7 us: on_device(): lax.psum((part_router, part_gain), 'expert')]
    all_to_all x1 -> x0, blocking collectives: 57.8 us -> none  [on_device(): lax.all_to_all(d_send.reshape(experts, capacity, width), 'expert', split_...]
    all_to_all x0 -> x1, waiting for transfers between devices: none -> 47.6 us  [on_device(): lax.all_to_all(d_send.reshape(experts, capacity, width), 'expert', split_...]
    all_to_all x1, waiting for transfers between devices: 43.3 us -> 0.01 us  [on_device(): lax.all_to_all(d_rows.reshape(experts, capacity, width), 'expert', split_...]
    all_to_all x0 -> x1, starting transfers between devices: none -> 8.84 us  [on_device(): lax.all_to_all(d_send.reshape(experts, capacity, width), 'expert', split_...]
    psum x1 -> x2, blocking collectives: 74.9 us -> 76.2 us  [the longest x1 63 us: on_device(): lax.psum((part_router, part_gain), 'expert')]
  transfers between devices with their start and end apart: 7 -> 9, of which waited for: 4 -> 5; matrix products, arithmetic and copies ran while one was open for 9% -> 18% of each run, Pallas kernels for 0% -> 0%
where the time goes in v1:
time: 534 us; the launch traced here: 527 us
  waiting for transfers between devices  228 us (43%)
  blocking collectives  136 us (25%)
  local copies, waits for them, and re-layouts  46.8 us (9%)
  matrix products  37 us (7%)
  other arithmetic  35 us (7%)
  starting transfers between devices  29.3 us (5%)
  between operations  14.8 us (3%)
    psum x1, blocking collectives, on_device(): lax.psum((part_router, part_gain), 'expert')  63 us
    all_to_all x1, blocking collectives, on_device(): lax.all_to_all(send_rows.reshape(experts, capacity, width), 'expert', spl...  60 us
    psum x1, waiting for transfers between devices, on_device(): lax.psum((part_router, part_gain), 'expert')  56.7 us
    psum x1, waiting for transfers between devices, on_device(): lax.psum(lax.psum((part_router, part_gain), 'expert'), 'dp')  50.8 us
    all_to_all x1, waiting for transfers between devices, on_device(): lax.all_to_all(d_send.reshape(experts, capacity, width), 'expert', split_...  47.6 us
    all_to_all x1, waiting for transfers between devices, on_device(): lax.all_to_all(expert_out.reshape(experts, capacity, width), 'expert', sp...  39.4 us
    all_gather x1, waiting for transfers between devices, on_device(): lax.all_gather(down_weight, 'dp', axis=2, tiled=True)[0]  31.2 us
    concatenate x1, other arithmetic, on_device(): jnp.concatenate([inner_product(expert_in, d_pre_gate), inner_product(expe...  21.4 us
  transfers between devices with their start and end apart: 9, of which 5 were waited for; matrix products, arithmetic and copies ran while one was open for 18% of the time, Pallas kernels for 0%

profile of v1, /device:TPU:2, one launch (start us, length us, event | category | flops | bytes accessed | tf_op | source)
XLA Modules:
  0.0 527.0 jit_solution(8401883406964677082)
XLA Ops:
  13.7 3.1 gather_fusion
  16.8 2.4 gather.20
  19.5 60.0 %all_to_all.20 = bf16[32,12,2048]{2,1,0:T(8,128)(2,1)S(1)} all-to-all(bf16[32,12,2048]{2,1,0:T(8,128)(2,1)S(1)} %broadcast_select_fusion), channel_id=1, replica_groups=mesh['dp'=8,'expert'=32] {'expert'}, dimensions={0} | all-to-all | bytes 3145728 | tf_op jit(solution)/shard_map/all_to_all | solution.py:58
  80.9 5.8 %fusion.10 = f32[384,1024]{1,0:T(8,128)} fusion(bf16[384,2048]{1,0:T(8,128)(2,1)} %reshape.196, bf16[1,2048,1024]{2,1,0:T(8,128)(2,1)} %all-gather.4.cloned.1.call-done), kind=kOutput, calls=%fused_computation.17 | convolution fusion | flops 1610612736 | bytes 7340032 | tf_op jit(solution)/shard_map/dot_general | solution.py:71
  86.6 6.0 %multiply_convert_fusion.2 = (bf16[384,1024]{1,0:T(8,128)(2,1)}, f32[384,1024]{1,0:T(8,128)}) fusion(f32[384,1024]{1,0:T(8,128)} %fusion.10, bf16[384,2048]{1,0:T(8,128)(2,1)S(1)} %copy-done.7, bf16[1,2048,1024]{2,1,0:T(8,128)(2,1)} %all-gather.6.cloned.1.call-done), kind=kOutput, calls=%fused_computation.31 | convolution fusion | flops 1612972032 | bytes 9699328 | tf_op jit(solution)/shard_map/dot_general | solution.py:72
  92.6 31.2 %all-gather.8.cloned.1.call-done = bf16[1,1024,2048]{2,1,0:T(8,128)(2,1)} async-done(((bf16[1,1024,256]{2,1,0:T(8,128)(2,1)}), bf16[1,1024,2048]{2,1,0:T(8,128)(2,1)}) %all-gather.8.cloned.1.call-update) | async-done | bytes 4194320 | tf_op jit(solution)/shard_map/all_gather | solution.py:78
  123.9 4.2 fusion.14
  129.7 10.8 %all-to-all-start.1 = ((bf16[32,12,2048]{2,1,0:T(8,128)(2,1)}), bf16[32,12,2048]{2,1,0:T(8,128)(2,1)}, u32[]{:S(2)}, u32[]{:S(2)}) async-start(bf16[32,12,2048]{2,1,0:T(8,128)(2,1)} %reshape.197), calls=%async_computation.1 | async-start | bytes 4194304 | tf_op jit(solution)/shard_map/all_to_all | solution.py:81
  140.7 3.3 gather_fusion.3
  144.0 4.6 gather.24
  148.9 39.4 %all-to-all-done.1 = bf16[32,12,2048]{2,1,0:T(8,128)(2,1)} async-done(((bf16[32,12,2048]{2,1,0:T(8,128)(2,1)}), bf16[32,12,2048]{2,1,0:T(8,128)(2,1)}, u32[]{:S(2)}, u32[]{:S(2)}) %all-to-all-start.1) | async-done | bytes 1572896 | tf_op jit(solution)/shard_map/all_to_all | solution.py:81
  188.3 2.5 reshape.198
  193.2 3.4 reshape.257
  196.6 2.6 multiply_reduce_fusion
  199.5 2.8 gather_fusion.2
  202.5 4.0 select_convert_fusion
  206.5 8.8 %all-to-all-start.2 = ((bf16[32,12,2048]{2,1,0:T(8,128)(2,1)}), bf16[32,12,2048]{2,1,0:T(8,128)(2,1)S(1)}, u32[]{:S(2)}, u32[]{:S(2)}) async-start(bf16[32,12,2048]{2,1,0:T(8,128)(2,1)} %select_convert_fusion), calls=%async_computation.2 | async-start | bytes 4194304 | tf_op jit(solution)/shard_map/all_to_all | solution.py:97
  217.0 47.6 %all-to-all-done.2 = bf16[32,12,2048]{2,1,0:T(8,128)(2,1)S(1)} async-done(((bf16[32,12,2048]{2,1,0:T(8,128)(2,1)}), bf16[32,12,2048]{2,1,0:T(8,128)(2,1)S(1)}, u32[]{:S(2)}, u32[]{:S(2)}) %all-to-all-start.2) | async-done | bytes 1572896 | tf_op jit(solution)/shard_map/all_to_all | solution.py:97
  266.0 4.1 convolution_convert_fusion
  272.6 2.4 convolution_convert_fusion.2
  275.0 2.4 convolution_convert_fusion.1
  277.4 21.4 %pad_maximum_fusion = bf16[2048,3072]{0,1:T(8,128)(2,1)} fusion(bf16[2048,1024]{0,1:T(8,128)(2,1)S(1)} %convolution_convert_fusion, bf16[2048,1024]{0,1:T(8,128)(2,1)S(1)} %convolution_convert_fusion.1, bf16[2048,1024]{0,1:T(8,128)(2,1)S(1)} %convolution_convert_fusion.2), kind=kLoop, calls=%fused_computation.6 | loop fusion | flops 37748736 | bytes 25165824 | tf_op jit(solution)/shard_map/concatenate | solution.py:118
  298.8 4.2 fusion.4
  306.4 8.9 %all-to-all-start.3 = ((bf16[32,12,2048]{2,1,0:T(8,128)(2,1)}), bf16[32,12,2048]{2,1,0:T(8,128)(2,1)}, u32[]{:S(2)}, u32[]{:S(2)}) async-start(bf16[32,12,2048]{2,1,0:T(8,128)(2,1)} %reshape.200), calls=%async_computation.3 | async-start | bytes 4194304 | tf_op jit(solution)/shard_map/all_to_all | solution.py:113
  315.4 2.6 copy_multiply_fusion
  318.0 56.7 %all-reduce.3.cloned.1.call-done = f32[2048,32]{0,1:T(8,128)} async-done(((f32[2048,32]{0,1:T(8,128)}), f32[2048,32]{0,1:T(8,128)}) %all-reduce.3.cloned.1.call-update) | async-done | bytes 262160 | tf_op jit(solution)/shard_map/psum | solution.py:148
  374.7 2.7 reshape.201
  381.8 2.4 fusion.31
  384.2 63.0 %psum.30 = f32[2048]{0:T(1024)S(1)} all-reduce(f32[2048]{0:T(1024)S(1)} %get-tuple-element.35), channel_id=1, replica_groups=mesh['dp'=8,'expert'=32] {'expert'}, use_global_device_ids=true, to_apply=%region_16.17 | all-reduce | flops 2048 | bytes 16384 | tf_op jit(solution)/shard_map/psum | solution.py:148
  447.2 13.2 %psum.31 = f32[2048]{0:T(1024)} all-reduce(f32[2048]{0:T(1024)S(1)} %psum.30), channel_id=1, replica_groups=mesh['dp'=8,'expert'=32] {'dp'}, use_global_device_ids=true, to_apply=%region_17.18 | all-reduce | flops 2048 | bytes 16384 | tf_op jit(solution)/shard_map/psum | solution.py:148
  460.4 2.7 fusion.30
  467.4 50.8 %all-reduce.5.cloned.1.call-done = f32[2048,32]{0,1:T(8,128)} async-done(((f32[2048,32]{0,1:T(8,128)}), f32[2048,32]{0,1:T(8,128)}) %all-reduce.5.cloned.1.call-update) | async-done | bytes 262160 | tf_op jit(solution)/shard_map/psum | solution.py:148
  (99 shorter events, 32.1 us)
Async XLA Ops:
  7.2 141.4 %copy-start = (bf16[2048,32]{0,1:T(8,128)(2,1)S(1)}, bf16[2048,32]{0,1:T(8,128)(2,1)}, u32[]{:S(2)}) copy-start(bf16[2048,32]{0,1:T(8,128)(2,1)} %param.12) | copy-start | bytes 393220
  7.2 6.1 %copy-start.3 = (bf16[128,2048]{1,0:T(8,128)(2,1)S(1)}, bf16[128,2048]{1,0:T(8,128)(2,1)}, u32[]{:S(2)}) copy-start(bf16[128,2048]{1,0:T(8,128)(2,1)} %param.8) | copy-start | bytes 1572868
  7.2 6.3 %copy-start.10 = (f32[2048]{0:T(1024)S(1)}, f32[2048]{0:T(1024)}, u32[]{:S(2)}) copy-start(f32[2048]{0:T(1024)} %param.11) | copy-start | bytes 24580
  7.2 73.7 %all-gather.4.cloned.1.call-start = ((), (), s32[]{:S(2)}) async-start(), calls=%async_computation.5 | async-start | bytes 4718592 | tf_op jit(solution)/shard_map/all_gather | solution.py:67
  7.9 78.7 %all-gather.6.cloned.1.call-start = ((), (), s32[]{:S(2)}) async-start(), calls=%async_computation.6 | async-start | bytes 4718592 | tf_op jit(solution)/shard_map/all_gather | solution.py:68
  8.7 115.2 %all-gather.8.cloned.1.call-start = ((), (), s32[]{:S(2)}) async-start(), calls=%async_computation.7 | async-start | bytes 4718592 | tf_op jit(solution)/shard_map/all_gather | solution.py:78
  80.9 5.8 %copy-start.7 = (bf16[384,2048]{1,0:T(8,128)(2,1)S(1)}, bf16[384,2048]{1,0:T(8,128)(2,1)}, u32[]{:S(2)}) copy-start(bf16[384,2048]{1,0:T(8,128)(2,1)} %reshape.196) | copy-start | bytes 4718596
  129.7 11.0 %copy-start.5 = (bf16[128,2048]{1,0:T(8,128)(2,1)S(1)}, bf16[128,2048]{1,0:T(8,128)(2,1)}, u32[]{:S(2)}) copy-start(bf16[128,2048]{1,0:T(8,128)(2,1)} %param.10) | copy-start | bytes 1572868
  129.7 58.7 %all-to-all-start.1 = ((bf16[32,12,2048]{2,1,0:T(8,128)(2,1)}), bf16[32,12,2048]{2,1,0:T(8,128)(2,1)}, u32[]{:S(2)}, u32[]{:S(2)}) async-start(bf16[32,12,2048]{2,1,0:T(8,128)(2,1)} %reshape.197), calls=%async_computation.1 | async-start | bytes 4194304 | tf_op jit(solution)/shard_map/all_to_all | solution.py:81
  144.0 4.9 copy-start.11
  206.5 58.2 %all-to-all-start.2 = ((bf16[32,12,2048]{2,1,0:T(8,128)(2,1)}), bf16[32,12,2048]{2,1,0:T(8,128)(2,1)S(1)}, u32[]{:S(2)}, u32[]{:S(2)}) async-start(bf16[32,12,2048]{2,1,0:T(8,128)(2,1)} %select_convert_fusion), calls=%async_computation.2 | async-start | bytes 4194304 | tf_op jit(solution)/shard_map/all_to_all | solution.py:97
  215.3 159.4 %all-reduce.3.cloned.1.call-start = ((), (), s32[]{:S(2)}) async-start(), calls=%async_computation.9 | async-start | bytes 524288 | tf_op jit(solution)/shard_map/psum | solution.py:148
  216.5 246.7 %reduce-scatter.2.cloned.1.call-start = ((), (), s32[]{:S(2)}) async-start(), calls=%async_computation.8 | async-start | bytes 14155776 | tf_op jit(solution)/shard_map/reduce_scatter | solution.py:117
  266.0 4.2 copy-start.9
  266.0 4.2 copy-start.13
  266.0 4.2 copy-start.14
  266.0 4.3 copy-start.15
  270.3 2.3 copy-start.8
  298.8 4.2 copy-start.12
  306.4 9.0 %copy-start.1 = (f32[128,2,2048]{2,1,0:T(2,128)S(1)}, f32[128,2,2048]{2,1,0:T(2,128)}, u32[]{:S(2)}) copy-start(f32[128,2,2048]{2,1,0:T(2,128)} %reshape.257) | copy-start | bytes 6291460
  306.4 68.3 %all-to-all-start.3 = ((bf16[32,12,2048]{2,1,0:T(8,128)(2,1)}), bf16[32,12,2048]{2,1,0:T(8,128)(2,1)}, u32[]{:S(2)}, u32[]{:S(2)}) async-start(bf16[32,12,2048]{2,1,0:T(8,128)(2,1)} %reshape.200), calls=%async_computation.3 | async-start | bytes 4194304 | tf_op jit(solution)/shard_map/all_to_all | solution.py:113
  315.3 202.9 %all-reduce.5.cloned.1.call-start = ((), (), s32[]{:S(2)}) async-start(), calls=%async_computation.10 | async-start | bytes 524288 | tf_op jit(solution)/shard_map/psum | solution.py:148
  380.1 1.7 copy-start.4
  381.8 78.7 %copy-start.2 = (f32[128,2,2048]{2,0,1:T(8,128)S(1)}, f32[128,2,2048]{2,0,1:T(8,128)}, u32[]{:S(2)}) copy-start(f32[128,2,2048]{2,0,1:T(8,128)} %copy_multiply_fusion) | copy-start | bytes 6291460
  381.8 78.6 %copy-start.6 = (bf16[128,2048]{1,0:T(8,128)(2,1)S(1)}, bf16[128,2048]{1,0:T(8,128)(2,1)}, u32[]{:S(2)}) copy-start(bf16[128,2048]{1,0:T(8,128)(2,1)} %param.10) | copy-start | bytes 1572868
Sparse Core Ops, SparseCore 0:
  9.9 37.5 all-gather.3
  49.3 34.5 all-gather.5
  85.8 38.0 all-gather.7
  219.8 154.7 all-reduce.2
  377.1 73.7 reduce-scatter.1
  453.0 65.1 all-reduce.4
